TPU v7x, 32 devices: a whole 2x2x4 slice. The times are simulated.
32 devices in a mesh: runs: 8 (over z, y), tp: 4 (over x, core).
Axes of the slice: x: 2, y: 2, z: 4, core: 2. Of those that a mesh axis runs over, the one named last changes fastest.
Arguments:
- hidden: bfloat16 [4096, 8192], P('runs', 'tp'), may hold values from -6 to 6
- cotangent: bfloat16 [4096, 8192], P('runs', 'tp'), may hold values from -0.059814453 to 0.059814453
- rotation: float32 [8192, 512], P(None, 'tp'), may hold values from -0.0625 to 0.0625
- matching: int32 [32], P('runs'), may hold values from 0 to 31
- mask: int32 [32, 128], P('runs'), may hold values 0 or 1
Outputs:
- intervened: bfloat16 [4096, 8192], P('runs', 'tp')
- grad_rotation: float32 [8192, 512], P('runs', 'tp')
All inputs are finite; a program needn't handle non-finite values. No bound on the sum of `mask` on one device may be relied on, other than what follows from the above.
Results may differ from a plain program's by a relative error of at most 0.0045.
Values may be sent and summed in bfloat16 or wider, within the bound.
A program may use at most 128 MiB of HBM per device.

v0:
```python
import jax
import jax.numpy as jnp
from jax import lax
from jax.sharding import PartitionSpec as P


def contract_tokens(left, right):
    return jnp.einsum(
        "td,tk->dk",
        left,
        right,
        precision=lax.Precision.HIGHEST,
        preferred_element_type=jnp.float32,
    )


def per_device(hidden, cotangent, rotation, matching, mask):
    high = lax.Precision.HIGHEST
    local_runs = matching.shape[0]
    length = mask.shape[1]
    columns = rotation.shape[1]
    peers = lax.axis_size("runs")
    full_hidden, full_cotangent = (
        lax.all_gather(hidden, "tp", axis=1, tiled=True),
        lax.all_gather(cotangent, "tp", axis=1, tiled=True),
    )
    coords = jnp.dot(full_hidden, rotation, precision=high, preferred_element_type=jnp.float32)
    own = coords.reshape(local_runs, length, columns)
    offsets = matching[:, None] * length + jnp.arange(length, dtype=jnp.int32)[None, :]
    piece = lax.all_gather(coords, "runs", axis=0, tiled=True)
    count = piece.shape[0]
    inside = (offsets >= 0) & (offsets < count)
    rows = jnp.take(piece, jnp.clip(offsets, 0, count - 1).reshape(-1), axis=0)
    rows = rows.reshape(local_runs, length, columns)
    picked = jnp.where(inside[:, :, None], rows, 0.0)
    chosen = mask.astype(jnp.float32)[:, :, None]
    update = (chosen * (picked - own)).reshape(local_runs * length, columns)
    own_rows = lax.all_to_all(rotation, "tp", split_axis=0, concat_axis=1, tiled=True)
    every_column = lax.all_gather(update, "tp", axis=1, tiled=True)
    added = jnp.dot(every_column, own_rows.T, precision=high, preferred_element_type=jnp.float32)
    intervened = (hidden.astype(jnp.float32) + added).astype(jnp.bfloat16)
    pulled = jnp.dot(full_cotangent, rotation, precision=high, preferred_element_type=jnp.float32)
    pulled = chosen * pulled.reshape(local_runs, length, columns)
    sources = jnp.arange(local_runs * lax.axis_size("runs"), dtype=jnp.int32)
    table = (sources[:, None] == matching[None, :]).astype(jnp.float32)
    returned = lax.psum_scatter(
        jnp.einsum("sb,blk->slk", table, pulled, precision=high).astype(jnp.bfloat16),
        "runs",
        scatter_dimension=0,
        tiled=True,
    ).astype(jnp.float32)
    net = (returned - pulled).reshape(local_runs * length, columns)
    term = contract_tokens(full_cotangent, update) + contract_tokens(full_hidden, net)
    total = lax.psum(term, "runs")
    share = term.shape[0] // peers
    grad_rotation = lax.dynamic_slice_in_dim(total, lax.axis_index("runs") * share, share, 0)
    return (intervened, grad_rotation)


def solution(mesh):
    in_specs = (P("runs", "tp"), P("runs", "tp"), P(None, "tp"), P("runs"), P("runs", None))
    out_specs = (P("runs", "tp"), P("runs", "tp"))
    return jax.shard_map(
        per_device, mesh=mesh, in_specs=in_specs, out_specs=out_specs, check_vma=False
    )
```

profile of v0, /device:TPU:29, one launch (start us, length us, event | category | flops | bytes accessed | tf_op | source)
XLA Modules:
  0.0 431.6 jit_solution(8518949762812222315)
XLA Ops:
  7.2 0.0 all-gather.5.cloned.1.call-start
  7.2 0.7 all-gather.5.cloned.1.call-update
  7.9 0.0 all-gather.11.cloned.1.call-start
  7.9 0.7 all-gather.11.cloned.1.call-update
  8.7 0.0 all-gather.7.cloned.1.call-start
  8.7 60.5 %all-gather.5.cloned.1.call-done = bf16[512,8192]{1,0:T(8,128)(2,1)} async-done(((bf16[512,2048]{1,0:T(8,128)(2,1)}), bf16[512,8192]{1,0:T(8,128)(2,1)}) %all-gather.5.cloned.1.call-update) | async-done | bytes 8388624 | tf_op jit(solution)/shard_map/all_gather | solution.py:24
  69.2 10.5 %fusion.11 = f32[512,128]{1,0:T(8,128)} fusion(bf16[512,8192]{1,0:T(8,128)(2,1)} %all-gather.5.cloned.1.call-done, f32[8192,128]{1,0:T(8,128)} %param.7), kind=kOutput, calls=%fused_computation.26 | convolution fusion | flops 6442450944 | bytes 12845056 | tf_op jit(solution)/shard_map/dot_general | solution.py:27
  79.7 0.0 reduce-scatter.2.cloned.1.call-start
  79.7 49.3 %all-gather.11.cloned.1.call-done = bf16[512,8192]{1,0:T(8,128)(2,1)} async-done(((bf16[512,2048]{1,0:T(8,128)(2,1)}), bf16[512,8192]{1,0:T(8,128)(2,1)}) %all-gather.11.cloned.1.call-update) | async-done | bytes 8388624 | tf_op jit(solution)/shard_map/all_gather | solution.py:25
  129.0 9.8 %fusion.13 = f32[512,128]{1,0:T(8,128)S(1)} fusion(bf16[512,8192]{1,0:T(8,128)(2,1)} %all-gather.11.cloned.1.call-done, f32[8192,128]{1,0:T(8,128)} %param.7), kind=kOutput, calls=%fused_computation.28 | convolution fusion | flops 6442450944 | bytes 12845056 | tf_op jit(solution)/shard_map/dot_general | solution.py:42
  138.8 0.1 broadcast_multiply_fusion
  139.0 1.1 convolution_convert_fusion
  140.1 1.4 copy.21
  141.5 0.0 all-gather.9.cloned.1.call-start
  141.6 0.1 fusion.2
  141.7 0.1 compare_and_fusion
  141.7 0.1 fusion.6
  141.8 35.7 %all-gather.7.cloned.1.call-done = f32[4096,128]{1,0:T(8,128)} async-done(((f32[512,128]{1,0:T(8,128)}), f32[4096,128]{1,0:T(8,128)}) %all-gather.7.cloned.1.call-update) | async-done | bytes 2097168 | tf_op jit(solution)/shard_map/all_gather | solution.py:30
  177.5 2.6 gather_fusion
  180.1 1.0 subtract_multiply_fusion
  181.1 0.2 all-reduce.2.cloned.1.call-start
  181.4 61.9 %reduce-scatter.2.cloned.1.call-done = bf16[4,128,128]{2,1,0:T(8,128)(2,1)} async-done(((bf16[32,128,128]{2,1,0:T(8,128)(2,1)}), bf16[4,128,128]{2,1,0:T(8,128)(2,1)}) %reduce-scatter.2.cloned.1.call-update) | async-done | bytes 131088 | tf_op jit(solution)/shard_map/reduce_scatter | solution.py:46
  243.2 1.0 convert_subtract_fusion
  244.3 6.0 %fusion.12 = f32[128,8192]{1,0:T(8,128)S(1)} fusion(f32[512,128]{1,0:T(8,128)} %subtract_multiply_fusion, bf16[512,8192]{1,0:T(8,128)(2,1)} %all-gather.11.cloned.1.call-done), kind=kOutput, calls=%fused_computation.27 | convolution fusion | flops 6442450944 | bytes 12845056 | tf_op jit(solution)/shard_map/td,tk->dk/dot_general | solution.py:8
  250.3 9.2 %fusion = f32[8192,128]{0,1:T(8,128)} fusion(f32[128,8192]{1,0:T(8,128)S(1)} %fusion.12, f32[512,128]{1,0:T(8,128)S(1)} %bitcast.34, bf16[512,8192]{1,0:T(8,128)(2,1)} %all-gather.5.cloned.1.call-done), kind=kOutput, calls=%fused_computation.2 | convolution fusion | flops 6443499520 | bytes 17039360 | tf_op jit(solution)/shard_map/td,tk->dk/dot_general | solution.py:8
  259.5 7.5 %all-to-all-start = ((f32[4,2048,128]{2,1,0:T(8,128)}), f32[4,2048,128]{2,1,0:T(8,128)}, u32[]{:S(2)}, u32[]{:S(2)}) async-start(f32[4,2048,128]{2,1,0:T(8,128)} %bitcast.30), calls=%async_computation | async-start | bytes 8388608 | tf_op jit(solution)/shard_map/all_to_all | solution.py:38
  267.0 47.3 %all-to-all-done = f32[4,2048,128]{2,1,0:T(8,128)} async-done(((f32[4,2048,128]{2,1,0:T(8,128)}), f32[4,2048,128]{2,1,0:T(8,128)}, u32[]{:S(2)}, u32[]{:S(2)}) %all-to-all-start) | async-done | bytes 4194336 | tf_op jit(solution)/shard_map/all_to_all | solution.py:38
  314.3 5.6 %copy.19 = f32[2048,4,128]{0,2,1:T(8,128)} copy(f32[2048,4,128]{2,0,1:T(8,128)} %bitcast.6) | data formatting | bytes 8388608 | tf_op jit(solution)/shard_map/all_to_all | solution.py:38
  319.9 10.0 %add_convert_fusion = bf16[512,2048]{1,0:T(8,128)(2,1)} fusion(bf16[512,2048]{1,0:T(8,128)(2,1)S(1)} %copy-done, f32[512,512]{1,0:T(8,128)} %all-gather.9.cloned.1.call-done, f32[2048,512]{0,1:T(8,128)} %bitcast.31), kind=kOutput, calls=%fused_computation.3 | convolution fusion | flops 6445596672 | bytes 9437184 | tf_op jit(solution)/shard_map/dot_general | solution.py:40
  329.9 92.7 %all-reduce.2.cloned.1.call-done = f32[8192,128]{0,1:T(8,128)} async-done(((f32[8192,128]{0,1:T(8,128)}), f32[8192,128]{0,1:T(8,128)}) %all-reduce.2.cloned.1.call-update) | async-done | bytes 4194320 | tf_op jit(solution)/shard_map/psum | solution.py:54
  422.6 1.1 constant_dynamic-slice_fusion
  423.7 1.0 copy.22
  (17 shorter events, 0.1 us)
Async XLA Ops:
  7.2 62.0 %all-gather.5.cloned.1.call-start = ((), (), s32[]{:S(2)}) async-start(), calls=%async_computation.2 | async-start | bytes 10485760 | tf_op jit(solution)/shard_map/all_gather | solution.py:24
  7.9 121.1 %all-gather.11.cloned.1.call-start = ((), (), s32[]{:S(2)}) async-start(), calls=%async_computation.5 | async-start | bytes 10485760 | tf_op jit(solution)/shard_map/all_gather | solution.py:25
  8.6 71.1 %copy-start.2 = (s32[4,128]{1,0:T(4,128)S(1)}, s32[4,128]{1,0:T(4,128)}, u32[]{:S(2)}) copy-start(s32[4,128]{1,0:T(4,128)} %param.9) | copy-start | bytes 6148
  8.7 168.8 %all-gather.7.cloned.1.call-start = ((), (), s32[]{:S(2)}) async-start(), calls=%async_computation.3 | async-start | bytes 2359296 | tf_op jit(solution)/shard_map/all_gather | solution.py:30
  79.7 163.5 %reduce-scatter.2.cloned.1.call-start = ((), (), s32[]{:S(2)}) async-start(), calls=%async_computation.6 | async-start | bytes 1179648 | tf_op jit(solution)/shard_map/reduce_scatter | solution.py:46
  79.7 59.2 %copy-start.3 = (s32[4]{0:T(128)S(1)}, s32[4]{0:T(128)}, u32[]{:S(2)}) copy-start(s32[4]{0:T(128)} %param.8) | copy-start | bytes 52
  138.8 41.3 %copy-start.1 = (f32[512,128]{1,0:T(8,128)S(1)}, f32[512,128]{1,0:T(8,128)}, u32[]{:S(2)}) copy-start(f32[512,128]{1,0:T(8,128)} %fusion.11) | copy-start | bytes 786436
  141.5 178.4 %all-gather.9.cloned.1.call-start = ((), (), s32[]{:S(2)}) async-start(), calls=%async_computation.4 | async-start | bytes 1310720 | tf_op jit(solution)/shard_map/all_gather | solution.py:39
  181.1 241.5 %all-reduce.2.cloned.1.call-start = ((), (), s32[]{:S(2)}) async-start(), calls=%async_computation.7 | async-start | bytes 8388608 | tf_op jit(solution)/shard_map/psum | solution.py:54
  259.5 54.7 %all-to-all-start = ((f32[4,2048,128]{2,1,0:T(8,128)}), f32[4,2048,128]{2,1,0:T(8,128)}, u32[]{:S(2)}, u32[]{:S(2)}) async-start(f32[4,2048,128]{2,1,0:T(8,128)} %bitcast.30), calls=%async_computation | async-start | bytes 8388608 | tf_op jit(solution)/shard_map/all_to_all | solution.py:38
  314.3 5.6 %copy-start = (bf16[512,2048]{1,0:T(8,128)(2,1)S(1)}, bf16[512,2048]{1,0:T(8,128)(2,1)}, u32[]{:S(2)}) copy-start(bf16[512,2048]{1,0:T(8,128)(2,1)} %param.5) | copy-start | bytes 6291460
Sparse Core Ops, SparseCore 0:
  9.5 59.5 all-gather.4
  70.7 58.2 all-gather.10
  131.7 45.7 all-gather.6
  181.3 61.8 reduce-scatter.1
  245.2 19.8 all-gather.8
  268.7 153.9 all-reduce.1
where the time goes:
time: 436 us; the launch traced here: 432 us
  waiting for transfers between devices  349 us (80%)
  matrix products  46.6 us (11%)
  between operations  14.2 us (3%)
  local copies, waits for them, and re-layouts  11.7 us (3%)
  starting transfers between devices  7.89 us (2%)
    psum x1, waiting for transfers between devices, per_device(): total = lax.psum(term, 'runs')  92.7 us
    reduce_scatter x1, waiting for transfers between devices, per_device(): lax.psum_scatter(jnp.einsum('sb,blk->slk', table, pulled, precision=high)...  61.9 us
    all_gather x1, waiting for transfers between devices, per_device(): lax.all_gather(hidden, 'tp', axis=1, tiled=True)  60.5 us
    all_gather x1, waiting for transfers between devices, per_device(): lax.all_gather(cotangent, 'tp', axis=1, tiled=True)  49.3 us
    all_to_all x1, waiting for transfers between devices, per_device(): lax.all_to_all(rotation, 'tp', split_axis=0, concat_axis=1, tiled=True)  47.3 us
    all_gather x1, waiting for transfers between devices, per_device(): piece = lax.all_gather(coords, 'runs', axis=0, tiled=True)  35.7 us
    dot_general x2, matrix products, contract_tokens(): jnp.einsum('td,tk->dk', left, right, precision=lax.Precision.HIGHEST, pre...  15.3 us
    dot_general x1, matrix products, per_device(): jnp.dot(full_hidden, rotation, precision=high, preferred_element_type=jnp...  10.5 us
  transfers between devices with their start and end apart: 7, of which 6 were waited for; matrix products, arithmetic and copies ran while one was open for 14% of the time, Pallas kernels for 0%

commit v1 on v0

v1 whole, which is shorter than its diff:
```python
import functools

import jax
import jax.numpy as jnp
from jax import lax
from jax.experimental import pallas as pl
from jax.experimental.pallas import tpu as pltpu
from jax.sharding import PartitionSpec as P

F32 = jnp.float32
BF16 = jnp.bfloat16


def kernel(
    R, T, lr, L, rows, hid, cot, rot, mask, matv, match, out, grad,
    x, w, part, prec, own, gath, matg, upd, gkeep, gsend, yrec, zsend, zrec, fin, frec,
    lsem, rsend, rrecv, msend, mrecv, psend, precv, asend, arecv, usend, urecv,
    ysend, yrecv, zsem, zrsem, fsem,
):
    q = R // T
    n, F = hid.shape
    C = rot.shape[1]
    S = F // q
    r = lax.axis_index("runs")
    j = lax.axis_index("tp")
    a = r // q
    b = lax.rem(r, q)
    blk = 2 * lr

    def remote(src, dst, ss, rs, dr, dj):
        return pltpu.make_async_remote_copy(
            src_ref=src, dst_ref=dst, send_sem=ss, recv_sem=rs,
            device_id=(dr, dj), device_id_type=pl.DeviceIdType.MESH,
        )

    def other(i, k, size):
        return lax.rem(i + k, size)

    loads = [
        pltpu.make_async_copy(hid, x.at[0], lsem.at[0]),
        pltpu.make_async_copy(cot, x.at[1], lsem.at[1]),
        pltpu.make_async_copy(
            rot.at[pl.ds(pl.multiple_of(j * F, F), F), :],
            w.at[:, pl.ds(pl.multiple_of(j * C, C), C)], lsem.at[2]),
        pltpu.make_async_copy(matv, matg.at[r], lsem.at[3]),
    ]
    for c in loads:
        c.start()

    barrier = pltpu.get_barrier_semaphore()
    for k in range(1, R):
        pl.semaphore_signal(barrier, inc=1, device_id=(other(r, k, R), j),
                            device_id_type=pl.DeviceIdType.MESH)
    for k in range(1, T):
        pl.semaphore_signal(barrier, inc=1, device_id=(r, other(j, k, T)),
                            device_id_type=pl.DeviceIdType.MESH)

    @pl.when(a != j)
    def _():
        pl.semaphore_signal(barrier, inc=1, device_id=(j * q + b, a),
                            device_id_type=pl.DeviceIdType.MESH)
    pl.semaphore_wait(barrier, R - 1 + T - 1 + jnp.where(a != j, 1, 0).astype(jnp.int32))

    rcopies = []
    for k in range(1, T):
        p = other(j, k, T)
        rcopies.append(remote(
            rot.at[pl.ds(pl.multiple_of(p * F, F), F), :],
            w.at[:, pl.ds(pl.multiple_of(j * C, C), C)],
            rsend.at[p], rrecv.at[j], r, p))
    for c in rcopies:
        c.start()
    mcopies = []
    for k in range(1, R):
        p = other(r, k, R)
        mcopies.append(remote(matv, matg.at[r], msend.at[p], mrecv.at[r], p, j))
    for c in mcopies:
        c.start()
    for c in loads:
        c.wait()
    for k in range(1, T):
        p = other(j, k, T)
        dst = w.at[:, pl.ds(pl.multiple_of(p * C, C), C)]
        remote(rot.at[pl.ds(0, F), :], dst, rsend.at[p], rrecv.at[p], r, p).wait_recv()

    step = L
    for s in range(2):
        def body(i, _, s=s):
            rs = pl.ds(pl.multiple_of(i * step, step), step)
            v = jnp.dot(x[s, rs, :], w[...], preferred_element_type=F32)
            ws = pl.ds(pl.multiple_of(s * n + i * step, step), step)
            for p in range(T):
                part[p, ws, :] = v[:, p * C:(p + 1) * C].astype(BF16)
                @pl.when(j == p)
                def _():
                    own[ws, :] = v[:, p * C:(p + 1) * C]
            return 0
        lax.fori_loop(0, n // step, body, 0)
    pcopies = []
    for k in range(1, T):
        p = other(j, k, T)
        pcopies.append(remote(part.at[p], prec.at[j], psend.at[p], precv.at[j], r, p))
    for c in pcopies:
        c.start()
    for k in range(1, T):
        p = other(j, k, T)
        remote(part.at[p], prec.at[p], psend.at[p], precv.at[p], r, p).wait_recv()
    for i in range(blk):
        rs = pl.ds(i * L, L)
        v = own[rs, :]
        for k in range(1, T):
            v = v + prec[other(j, k, T), rs, :].astype(F32)
        if i >= lr:
            v = v * mask[pl.ds((i - lr) * L, L), :]
        own[rs, :] = v
        gath[r * blk + i] = v.astype(BF16)

    def block(g):
        return gath.at[pl.ds(g * blk, blk)]

    sends = []
    for k in range(1, T):
        p = other(a, k, T)
        sends.append(remote(block(r), block(r), asend.at[p, b], arecv.at[r], p * q + b, j))
    for k in range(1, q):
        p = other(b, k, q)
        sends.append(remote(block(r), block(r), asend.at[a, p], arecv.at[r], a * q + p, j))
    for c in sends:
        c.start()
    for k in range(1, T):
        p = other(a, k, T)
        g = p * q + b
        remote(block(g), block(g), asend.at[p, b], arecv.at[g], g, j).wait_recv()
        for m in range(1, q):
            e = other(b, m, q)
            c = remote(block(g), block(g), asend.at[p, e], arecv.at[g], a * q + e, j)
            c.start()
            sends.append(c)
    for k in range(T):
        p = other(a, k, T)
        for m in range(1, q):
            g = p * q + other(b, m, q)
            remote(block(g), block(g), asend.at[p, b], arecv.at[g], g, j).wait_recv()
    for k in range(1, R):
        p = other(r, k, R)
        remote(matv, matg.at[p], msend.at[p], mrecv.at[p], p, j).wait_recv()

    for i in range(lr):
        rs = pl.ds(i * L, L)
        m = match[i]
        src = gath[m + (m // lr) * lr].astype(F32)
        mine = matg[r, pl.ds(i, 1), :] == (r * lr + i).astype(F32)
        upd[j, rs, :] = jnp.where(mine, 0.0, mask[rs, :] * (src - own[rs, :])).astype(BF16)

        def back(g, acc, i=i):
            for u in range(lr):
                hit = matg[g, pl.ds(u, 1), :] == (r * lr + i).astype(F32)
                acc = acc + jnp.where(hit, gath[g * blk + lr + u].astype(F32), 0.0)
            return acc
        acc = lax.fori_loop(0, R, back, -own[pl.ds((lr + i) * L, L), :])
        for u in range(lr):
            hit = matg[r, pl.ds(u, 1), :] == (r * lr + i).astype(F32)
            full = own[pl.ds((lr + u) * L, L), :]
            acc = acc + jnp.where(hit, full - gath[r * blk + lr + u].astype(F32), 0.0)
        upd[j, pl.ds(n + i * L, L), :] = acc.astype(BF16)
    ucopies = []
    for k in range(1, T):
        p = other(j, k, T)
        ucopies.append(remote(upd.at[j], upd.at[j], usend.at[p], urecv.at[j], r, p))
    for c in ucopies:
        c.start()

    def grads(p):
        def half(e):
            fs = pl.ds(pl.multiple_of(e * S, S), S)
            dims = (((0,), (0,)), ((), ()))
            return (
                lax.dot_general(upd[p, pl.ds(0, n), :], x[1, :, fs], dims, preferred_element_type=F32)
                + lax.dot_general(upd[p, pl.ds(n, n), :], x[0, :, fs], dims, preferred_element_type=F32))
        gkeep[p] = half(b)
        for m in range(1, q):
            e = other(b, m, q)
            gsend[p, e] = half(e).astype(BF16)
            c = remote(gsend.at[p, e], yrec.at[b, p], ysend.at[p, e], yrecv.at[b, p], a * q + e, j)
            c.start()

    order = [other(j, k, T) for k in range(T)]
    for k, p in enumerate(order):
        if k:
            remote(upd.at[p], upd.at[p], usend.at[p], urecv.at[p], r, p).wait_recv()
        grads(p)

    def inter(i, _):
        rs = pl.ds(pl.multiple_of(i * L, L), L)
        u = jnp.concatenate([upd[p, rs, :] for p in range(T)], axis=1)
        v = lax.dot_general(u, w[...], (((1,), (1,)), ((), ())), preferred_element_type=F32)
        out[rs, :] = (x[0, rs, :].astype(F32) + v).astype(BF16)
        return 0

    def ysum(p):
        v = gkeep[p]
        for m in range(1, q):
            e = other(b, m, q)
            remote(gsend.at[p, e], yrec.at[e, p], ysend.at[p, e], yrecv.at[e, p], a * q + e, j).wait_recv()
            v = v + yrec[e, p].astype(F32)
        return v

    for p in order:
        v = ysum(p)

        @pl.when(p == a)
        def _():
            fin[...] = v

        @pl.when(p != a)
        def _():
            zsend[p] = v.astype(BF16)
            remote(zsend.at[p], zrec.at[a], zsem.at[p], zrsem.at[a], p * q + b, j).start()
    lax.fori_loop(0, n // L, inter, 0)
    for k in range(1, T):
        p = other(a, k, T)
        remote(zsend.at[p], zrec.at[p], zsem.at[p], zrsem.at[p], p * q + b, j).wait_recv()
    v = fin[...]
    for k in range(1, T):
        v = v + zrec[other(a, k, T)].astype(F32)
    fin[...] = v

    @pl.when(a != j)
    def _():
        c = remote(fin, frec, fsem.at[0], fsem.at[1], j * q + b, a)
        c.start()
        c.wait()
        grad[...] = frec[...].T

    @pl.when(a == j)
    def _():
        grad[...] = fin[...].T

    for c in rcopies + mcopies + pcopies + sends + ucopies:
        c.wait_send()
    for k in range(T):
        p = other(j, k, T)
        for m in range(1, q):
            e = other(b, m, q)
            remote(gsend.at[p, e], yrec.at[b, p], ysend.at[p, e], yrecv.at[b, p], a * q + e, j).wait_send()
    for k in range(1, T):
        p = other(a, k, T)
        remote(zsend.at[p], zrec.at[a], zsem.at[p], zrsem.at[a], p * q + b, j).wait_send()


def per_device(R, T, hidden, cotangent, rotation, matching, mask):
    n, F = hidden.shape
    D, C = rotation.shape
    lr, L = mask.shape
    q = R // T
    S = F // q
    rows = -(-lr // 8) * 8
    rot = rotation.astype(BF16)
    maskf = jnp.broadcast_to(mask.astype(F32).reshape(n, 1), (n, C))
    matv = jnp.broadcast_to(jnp.pad(matching, (0, rows - lr)).astype(F32)[:, None], (rows, C))
    dma = lambda *s: pltpu.SemaphoreType.DMA(s)
    any_, vm, sm = (pl.BlockSpec(memory_space=m) for m in (pl.ANY, pltpu.VMEM, pltpu.SMEM))
    return pl.pallas_call(
        functools.partial(kernel, R, T, lr, L, rows),
        out_shape=(
            jax.ShapeDtypeStruct((n, F), BF16),
            jax.ShapeDtypeStruct((S, C), F32),
        ),
        in_specs=[any_, any_, any_, vm, vm, sm],
        out_specs=(vm, vm),
        scratch_shapes=[
            pltpu.VMEM((2, n, F), BF16),
            pltpu.VMEM((F, T * C), BF16),
            pltpu.VMEM((T, 2 * n, C), BF16),
            pltpu.VMEM((T, 2 * n, C), BF16),
            pltpu.VMEM((2 * n, C), F32),
            pltpu.VMEM((R * 2 * lr, L, C), BF16),
            pltpu.VMEM((R, rows, C), F32),
            pltpu.VMEM((T, 2 * n, C), BF16),
            pltpu.VMEM((T, C, S), F32),
            pltpu.VMEM((T, q, C, S), BF16),
            pltpu.VMEM((q, T, C, S), BF16),
            pltpu.VMEM((T, C, S), BF16),
            pltpu.VMEM((T, C, S), BF16),
            pltpu.VMEM((C, S), F32),
            pltpu.VMEM((C, S), F32),
            dma(4), dma(T), dma(T), dma(R), dma(R), dma(T), dma(T),
            dma(T, q), dma(R), dma(T), dma(T),
            dma(T, q), dma(q, T), dma(T), dma(T), dma(2),
        ],
        compiler_params=pltpu.CompilerParams(
            collective_id=0, has_side_effects=True, vmem_limit_bytes=60 * 1024 * 1024
        ),
    )(hidden, cotangent, rot, maskf, matv, matching)


def solution(mesh):
    in_specs = (P("runs", "tp"), P("runs", "tp"), P(None, "tp"), P("runs"), P("runs", None))
    out_specs = (P("runs", "tp"), P("runs", "tp"))
    return jax.shard_map(
        functools.partial(per_device, mesh.shape["runs"], mesh.shape["tp"]),
        mesh=mesh, in_specs=in_specs, out_specs=out_specs, check_vma=False,
    )
```

time: 436 us -> 151 us (0.35)
  waiting for transfers between devices: 349 us -> 0 us
  Pallas kernels: 0 us -> 137 us
  matrix products: 46.6 us -> 0 us
  between operations: 14.2 us -> 0.65 us
  starting transfers between devices: 7.89 us -> 0 us
  local copies, waits for them, and re-layouts: 11.7 us -> 5.51 us
    all_gather x4 -> x0, waiting for transfers between devices: 145 us -> none  [the longest x1 60.5 us: per_device(): lax.all_gather(hidden, 'tp', axis=1, tiled=True)]
    pallas_call x0 -> x1, Pallas kernels: none -> 137 us  [per_device(): pl.pallas_call(functools.partial(kernel, R, T, lr, L, rows), out_shape=(j...]
    psum x1 -> x0, waiting for transfers between devices: 92.7 us -> none  [per_device(): total = lax.psum(term, 'runs')]
    reduce_scatter x1 -> x0, waiting for transfers between devices: 61.9 us -> none  [per_device(): lax.psum_scatter(jnp.einsum('sb,blk->slk', table, pulled, precision=high)...]
    all_to_all x1 -> x0, waiting for transfers between devices: 47.3 us -> none  [per_device(): lax.all_to_all(rotation, 'tp', split_axis=0, concat_axis=1, tiled=True)]
    dot_general x6 -> x0, matrix products: 46.6 us -> none  [the longest x2 15.3 us: contract_tokens(): jnp.einsum('td,tk->dk', left, right, precision=lax.Precision.HIGHEST, pre...]
    all_to_all x1 -> x0, starting transfers between devices: 7.47 us -> none  [per_device(): lax.all_to_all(rotation, 'tp', split_axis=0, concat_axis=1, tiled=True)]
    all_to_all x1 -> x0, local copies, waits for them, and re-layouts: 5.63 us -> none  [per_device(): lax.all_to_all(rotation, 'tp', split_axis=0, concat_axis=1, tiled=True)]
  transfers between devices with their start and end apart: 7 -> 0, of which waited for: 6 -> 0; matrix products, arithmetic and copies ran while one was open for 14% -> 0% of each run, Pallas kernels for 0% -> 0%
where the time goes in v1:
time: 151 us; the launch traced here: 148 us
  Pallas kernels  137 us (91%)
  local copies, waits for them, and re-layouts  5.51 us (4%)
  other arithmetic  5.05 us (3%)
    pallas_call x1, Pallas kernels, per_device(): pl.pallas_call(functools.partial(kernel, R, T, lr, L, rows), out_shape=(j...  137 us
    unnamed x4, local copies, waits for them, and re-layouts  4.01 us
    convert_element_type x1, other arithmetic, per_device(): rot = rotation.astype(BF16)  3.71 us

profile of v1, /device:TPU:29, one launch (start us, length us, event | category | flops | bytes accessed | tf_op | source)
XLA Modules:
  0.0 148.1 jit_solution(13872096405071502302)
XLA Ops:
  0.6 0.7 pad_convert_fusion
  1.3 0.7 convert_bitcast_fusion
  2.0 0.7 broadcast_in_dim.15.matv
  2.6 0.8 broadcast_in_dim.14.mask
  3.5 3.7 %convert_element_type.9.rot = bf16[8192,128]{1,0:T(8,128)(2,1)} convert(f32[8192,128]{1,0:T(8,128)} %param.7) | non-fusion elementwise | flops 1048576 | bytes 6291456 | tf_op jit(solution)/shard_map/convert_element_type | solution.py:258
  7.2 136.9 %shard_map.68 = (bf16[512,2048]{1,0:T(8,128)(2,1)}, f32[1024,128]{1,0:T(8,128)}) custom-call(bf16[512,2048]{1,0:T(8,128)(2,1)} %hid.1, bf16[512,2048]{1,0:T(8,128)(2,1)} %cot.1, bf16[8192,128]{1,0:T(8,128)(2,1)} %convert_element_type.9.rot, f32[512,128]{1,0:T(8,128)} %broadcast_in_dim.14.mask, f32[8,128]{1,0:T(8,128)} %broadcast_in_dim.15.matv, s32[4]{0:T(128)} %match.1), custom_call_target="tpu_custom_call" | custom-call | tf_op jit(solution)/shard_map/pallas_call | solution.py:263
  144.1 0.0 copy-start
  144.1 3.2 %copy.9 = bf16[512,2048]{1,0:T(8,128)(2,1)} copy(bf16[512,2048]{1,0:T(8,128)(2,1)} %get-tuple-element.4) | data formatting | bytes 4194304
  147.3 0.0 copy-done
  147.3 0.8 copy.10
Async XLA Ops:
  144.1 3.2 %copy-start = (f32[1024,128]{1,0:T(8,128)S(1)}, f32[1024,128]{1,0:T(8,128)}, u32[]{:S(2)}) copy-start(f32[1024,128]{1,0:T(8,128)} %get-tuple-element.5) | copy-start | bytes 1572868

commit v2 on v1

v2 whole, which is shorter than its diff:
```python
import functools

import jax
import jax.numpy as jnp
from jax import lax
from jax.experimental import pallas as pl
from jax.experimental.pallas import tpu as pltpu
from jax.sharding import PartitionSpec as P

F32 = jnp.float32
BF16 = jnp.bfloat16


def kernel(
    R, T, H, lr, L, hid, cot, rot, mask, matv, match, out, grad,
    x, w, part, prec, pfull, pfrec, own, gath, matg, upd, updt, gkeep, gsend, yrec, zsend, zrec, fin, frec,
    lsem, psem, rsend, rrecv, msend, mrecv, psend, precv, qsem, asend, arecv, usend, urecv,
    ysend, yrecv, zsem, zrsem, fsem,
):
    q = R // T
    n, F = hid.shape
    C = rot.shape[1]
    S = F // q
    r = lax.axis_index("runs")
    j = lax.axis_index("tp")
    a = r // q
    b = lax.rem(r, q)
    blk = 2 * lr

    def mate(i):
        return i + 1 - 2 * lax.rem(i, 2)

    partner = mate(j)

    def remote(src, dst, ss, rs, dr, dj):
        return pltpu.make_async_remote_copy(
            src_ref=src, dst_ref=dst, send_sem=ss, recv_sem=rs,
            device_id=(dr, dj), device_id_type=pl.DeviceIdType.MESH,
        )

    def other(i, k, size):
        return lax.rem(i + k, size)

    loads = [
        pltpu.make_async_copy(hid, x.at[0], lsem.at[0]),
        pltpu.make_async_copy(cot, x.at[1], lsem.at[1]),
        pltpu.make_async_copy(
            rot.at[pl.ds(pl.multiple_of(j * F, F), F), :],
            w.at[:, pl.ds(pl.multiple_of(j * C, C), C)], lsem.at[2]),
        pltpu.make_async_copy(matv, matg.at[r], lsem.at[3]),
    ]
    for c in loads:
        c.start()

    barrier = pltpu.get_barrier_semaphore()
    for k in range(1, R):
        pl.semaphore_signal(barrier, inc=1, device_id=(other(r, k, R), j),
                            device_id_type=pl.DeviceIdType.MESH)
    for k in range(1, T):
        pl.semaphore_signal(barrier, inc=1, device_id=(r, other(j, k, T)),
                            device_id_type=pl.DeviceIdType.MESH)

    @pl.when(a != j)
    def _():
        pl.semaphore_signal(barrier, inc=1, device_id=(j * q + b, a),
                            device_id_type=pl.DeviceIdType.MESH)
    pl.semaphore_wait(barrier, R - 1 + T - 1 + jnp.where(a != j, 1, 0).astype(jnp.int32))

    def wblock(g, row, size):
        return w.at[pl.ds(pl.multiple_of(row, size), size), pl.ds(pl.multiple_of(g * C, C), C)]

    def rrows(row, size):
        return rot.at[pl.ds(pl.multiple_of(row, size), size), :]

    sub = F // q // 2
    cross = []
    for k in range(1, T // 2):
        same = other(j, 2 * k, T)
        cross.append((same, mate(same)))
    far = [p for pair in cross for p in pair]
    rcopies = []
    for u in range(2):
        for p in far:
            at = b * (2 * sub) + u * sub
            rcopies.append(remote(
                rrows(p * F + at, sub), wblock(j, at, sub),
                rsend.at[p, b, u], rrecv.at[j, b, u], r, p))
    rcopies.append(remote(rrows(partner * F, F), wblock(j, 0, F), psem.at[0], psem.at[1], r, partner))
    for c in rcopies:
        c.start()
    mcopies = []
    for k in range(1, R):
        p = other(r, k, R)
        mcopies.append(remote(matv, matg.at[r], msend.at[p], mrecv.at[r], p, j))
    for c in mcopies:
        c.start()
    for u in range(2):
        for p in far:
            here = wblock(p, b * (2 * sub) + u * sub, sub)
            remote(here, here, rsend.at[p, b, u], rrecv.at[p, b, u], r, p).wait_recv()
            for m in range(1, q):
                e = other(b, m, q)
                c = remote(here, here, rsend.at[p, e, u], rrecv.at[p, b, u], a * q + e, j)
                c.start()
                rcopies.append(c)
    for c in loads:
        c.wait()
    remote(rrows(partner * F, F), wblock(partner, 0, F), psem.at[0], psem.at[1], r, partner).wait_recv()
    for u in range(2):
        for p in far:
            for m in range(1, q):
                e = other(b, m, q)
                here = wblock(p, e * (2 * sub) + u * sub, sub)
                remote(here, here, rsend.at[p, e, u], rrecv.at[p, e, u], a * q + e, j).wait_recv()

    step = L
    pcopies = []
    for s in range(2):
        def body(i, _, s=s):
            rs = pl.ds(pl.multiple_of(i * step, step), step)
            v = jnp.dot(x[s, rs, :], w[...], preferred_element_type=F32)
            ws = pl.ds(pl.multiple_of(s * n + i * step, step), step)
            for p in range(T):
                part[p, ws, :] = v[:, p * C:(p + 1) * C].astype(BF16)
                @pl.when(j == p)
                def _():
                    own[ws, :] = v[:, p * C:(p + 1) * C]
                @pl.when(partner == p)
                def _():
                    pfull[ws, :] = v[:, p * C:(p + 1) * C]
            return 0
        lax.fori_loop(0, n // step, body, 0)
        span = pl.ds(s * n, n)
        for p in far:
            pcopies.append(remote(part.at[p, span], prec.at[j, span], psend.at[p, s], precv.at[j, s], r, p))
            pcopies[-1].start()
        pcopies.append(remote(pfull.at[span], pfrec.at[span], qsem.at[0, s], qsem.at[1, s], r, partner))
        pcopies[-1].start()

    def block(g, s):
        return gath.at[pl.ds(g * blk + s * lr, lr)]

    sends = []
    for s in range(2):
        span = pl.ds(s * n, n)
        for p in far:
            remote(part.at[p, span], prec.at[p, span], psend.at[p, s], precv.at[p, s], r, p).wait_recv()
        remote(pfull.at[span], pfrec.at[span], qsem.at[0, s], qsem.at[1, s], r, partner).wait_recv()
        for i in range(lr):
            rs = pl.ds(s * n + i * L, L)
            v = own[rs, :] + pfrec[rs, :]
            for p in far:
                v = v + prec[p, rs, :].astype(F32)
            if s == 1:
                v = v * mask[pl.ds(i * L, L), :]
            own[rs, :] = v
            gath[r * blk + s * lr + i] = v.astype(BF16)
        for k in range(1, T):
            p = other(a, k, T)
            sends.append(remote(block(r, s), block(r, s), asend.at[p, b, s], arecv.at[r, s], p * q + b, j))
            sends[-1].start()
        for k in range(1, q):
            p = other(b, k, q)
            sends.append(remote(block(r, s), block(r, s), asend.at[a, p, s], arecv.at[r, s], a * q + p, j))
            sends[-1].start()
    for s in range(2):
        for k in range(1, T):
            p = other(a, k, T)
            g = p * q + b
            remote(block(g, s), block(g, s), asend.at[p, b, s], arecv.at[g, s], g, j).wait_recv()
            for m in range(1, q):
                e = other(b, m, q)
                c = remote(block(g, s), block(g, s), asend.at[p, e, s], arecv.at[g, s], a * q + e, j)
                c.start()
                sends.append(c)
    for s in range(2):
        for k in range(T):
            p = other(a, k, T)
            for m in range(1, q):
                g = p * q + other(b, m, q)
                remote(block(g, s), block(g, s), asend.at[p, b, s], arecv.at[g, s], g, j).wait_recv()
    for k in range(1, R):
        p = other(r, k, R)
        remote(matv, matg.at[p], msend.at[p], mrecv.at[p], p, j).wait_recv()

    for i in range(lr):
        rs = pl.ds(i * L, L)
        m = match[i]
        src = gath[m + (m // lr) * lr].astype(F32)
        mine = matg[r, pl.ds(i, 1), :] == (r * lr + i).astype(F32)
        upd[j, rs, :] = jnp.where(mine, 0.0, mask[rs, :] * (src - own[rs, :])).astype(BF16)

        def back(g, acc, i=i):
            for u in range(lr):
                hit = matg[g, pl.ds(u, 1), :] == (r * lr + i).astype(F32)
                acc = acc + jnp.where(hit, gath[g * blk + lr + u].astype(F32), 0.0)
            return acc
        acc = lax.fori_loop(0, R, back, -own[pl.ds((lr + i) * L, L), :])
        for u in range(lr):
            hit = matg[r, pl.ds(u, 1), :] == (r * lr + i).astype(F32)
            full = own[pl.ds((lr + u) * L, L), :]
            acc = acc + jnp.where(hit, full - gath[r * blk + lr + u].astype(F32), 0.0)
        upd[j, pl.ds(n + i * L, L), :] = acc.astype(BF16)

    def pass_on(g, k, way, dj):
        return remote(upd.at[g], upd.at[g], usend.at[way, k], urecv.at[g], r, dj)

    ucopies = [pass_on(j, p, 0, p) for p, _ in cross] + [pass_on(j, partner, 0, partner)]
    for c in ucopies:
        c.start()

    Sh = S // H

    def half(p, e, h):
        fs = pl.ds(pl.multiple_of(e * S + h * Sh, Sh), Sh)
        return (
            jnp.dot(updt[p, :, pl.ds(0, n)], x[1, :, fs], preferred_element_type=F32)
            + jnp.dot(updt[p, :, pl.ds(n, n)], x[0, :, fs], preferred_element_type=F32))

    def ysend_of(p, e, h):
        return remote(gsend.at[p, e, h], yrec.at[b, p, h], ysend.at[p, e, h], yrecv.at[b, p, h], a * q + e, j)

    def grads(p, h):
        for m in range(1, q):
            e = other(b, m, q)
            gsend[p, e, h] = half(p, e, h).astype(BF16)
            ysend_of(p, e, h).start()
        gkeep[p, h] = half(p, b, h)

    def arrive(g):
        pass_on(g, g, 0, j).wait_recv()
        updt[g] = upd[g].T

    updt[j] = upd[j].T
    for h in range(H):
        grads(j, h)
    arrive(partner)
    grads(partner, 0)
    for same, _ in cross:
        pass_on(same, same, 0, j).wait_recv()
        c = pass_on(same, same, 1, partner)
        c.start()
        ucopies.append(c)
        updt[same] = upd[same].T
        grads(same, 0)
    for _, p in cross:
        arrive(p)
        grads(p, 0)
    rest = [partner] + [p for p, _ in cross] + [p for _, p in cross]
    for h in range(1, H):
        for p in rest:
            grads(p, h)

    def inter(i, _):
        rs = pl.ds(pl.multiple_of(i * L, L), L)
        u = jnp.concatenate([upd[p, rs, :] for p in range(T)], axis=1)
        v = lax.dot_general(u, w[...], (((1,), (1,)), ((), ())), preferred_element_type=F32)
        out[rs, :] = (x[0, rs, :].astype(F32) + v).astype(BF16)
        return 0

    def zsend_of(p, h):
        return remote(zsend.at[p, h], zrec.at[a, h], zsem.at[p, h], zrsem.at[a, h], p * q + b, j)

    def ysum(p, h):
        v = gkeep[p, h]
        for m in range(1, q):
            e = other(b, m, q)
            remote(gsend.at[p, e, h], yrec.at[e, p, h], ysend.at[p, e, h], yrecv.at[e, p, h], a * q + e, j).wait_recv()
            v = v + yrec[e, p, h].astype(F32)

        @pl.when(p == a)
        def _():
            fin[h] = v

        @pl.when(p != a)
        def _():
            zsend[p, h] = v.astype(BF16)
            zsend_of(p, h).start()

    def move(h):
        return remote(fin.at[h], frec.at[h], fsem.at[0, h], fsem.at[1, h], j * q + b, a)

    def total(h):
        v = fin[h]
        for k in range(1, T):
            p = other(a, k, T)
            remote(zsend.at[p, h], zrec.at[p, h], zsem.at[p, h], zrsem.at[p, h], p * q + b, j).wait_recv()
            v = v + zrec[p, h].astype(F32)
        fin[h] = v

        @pl.when(a != j)
        def _():
            move(h).start()

    for h in range(H):
        ysum(j, h)
    lax.fori_loop(0, n // L, inter, 0)
    for h in range(H):
        for p in rest:
            ysum(p, h)
        if h:
            total(h - 1)
    total(H - 1)

    for h in range(H):
        @pl.when(a != j)
        def _(h=h):
            move(h).wait()
            grad[pl.ds(h * Sh, Sh), :] = frec[h].T

        @pl.when(a == j)
        def _(h=h):
            grad[pl.ds(h * Sh, Sh), :] = fin[h].T

    for c in rcopies + mcopies + pcopies + sends + ucopies:
        c.wait_send()
    for h in range(H):
        for k in range(T):
            for m in range(1, q):
                ysend_of(other(j, k, T), other(b, m, q), h).wait_send()
        for k in range(1, T):
            zsend_of(other(a, k, T), h).wait_send()


def per_device(R, T, hidden, cotangent, rotation, matching, mask):
    n, F = hidden.shape
    D, C = rotation.shape
    lr, L = mask.shape
    q = R // T
    S = F // q
    H = max(1, min(4, S // 128))
    rows = -(-lr // 8) * 8
    rot = rotation.astype(BF16)
    maskf = jnp.broadcast_to(mask.astype(F32).reshape(n, 1), (n, C))
    matv = jnp.broadcast_to(jnp.pad(matching, (0, rows - lr)).astype(F32)[:, None], (rows, C))
    dma = lambda *s: pltpu.SemaphoreType.DMA(s)
    any_, vm, sm = (pl.BlockSpec(memory_space=m) for m in (pl.ANY, pltpu.VMEM, pltpu.SMEM))
    return pl.pallas_call(
        functools.partial(kernel, R, T, H, lr, L),
        out_shape=(
            jax.ShapeDtypeStruct((n, F), BF16),
            jax.ShapeDtypeStruct((S, C), F32),
        ),
        in_specs=[any_, any_, any_, vm, vm, sm],
        out_specs=(vm, vm),
        scratch_shapes=[
            pltpu.VMEM((2, n, F), BF16),
            pltpu.VMEM((F, T * C), BF16),
            pltpu.VMEM((T, 2 * n, C), BF16),
            pltpu.VMEM((T, 2 * n, C), BF16),
            pltpu.VMEM((2 * n, C), F32),
            pltpu.VMEM((2 * n, C), F32),
            pltpu.VMEM((2 * n, C), F32),
            pltpu.VMEM((R * 2 * lr, L, C), BF16),
            pltpu.VMEM((R, rows, C), F32),
            pltpu.VMEM((T, 2 * n, C), BF16),
            pltpu.VMEM((T, C, 2 * n), BF16),
            pltpu.VMEM((T, H, C, S // H), F32),
            pltpu.VMEM((T, q, H, C, S // H), BF16),
            pltpu.VMEM((q, T, H, C, S // H), BF16),
            pltpu.VMEM((T, H, C, S // H), BF16),
            pltpu.VMEM((T, H, C, S // H), BF16),
            pltpu.VMEM((H, C, S // H), F32),
            pltpu.VMEM((H, C, S // H), F32),
            dma(4), dma(2), dma(T, q, 2), dma(T, q, 2), dma(R), dma(R),
            dma(T, 2), dma(T, 2), dma(2, 2),
            dma(T, q, 2), dma(R, 2), dma(2, T), dma(T),
            dma(T, q, H), dma(q, T, H), dma(T, H), dma(T, H), dma(2, H),
        ],
        compiler_params=pltpu.CompilerParams(
            collective_id=0, has_side_effects=True, vmem_limit_bytes=60 * 1024 * 1024
        ),
    )(hidden, cotangent, rot, maskf, matv, matching)


def solution(mesh):
    in_specs = (P("runs", "tp"), P("runs", "tp"), P(None, "tp"), P("runs"), P("runs", None))
    out_specs = (P("runs", "tp"), P("runs", "tp"))
    return jax.shard_map(
        functools.partial(per_device, mesh.shape["runs"], mesh.shape["tp"]),
        mesh=mesh, in_specs=in_specs, out_specs=out_specs, check_vma=False,
    )
```

time: 151 us -> 137 us (0.907); the launches traced: 148 us -> 136 us
  Pallas kernels: 137 us -> 125 us
    pallas_call x1, Pallas kernels: 137 us -> 125 us  [per_device(): pl.pallas_call(functools.partial(kernel, R, T, H, lr, L), out_shape=(jax....]
where the time goes in v2:
time: 137 us; the launch traced here: 136 us
  Pallas kernels  125 us (91%)
  local copies, waits for them, and re-layouts  5.51 us (4%)
  other arithmetic  5.05 us (4%)
    pallas_call x1, Pallas kernels, per_device(): pl.pallas_call(functools.partial(kernel, R, T, H, lr, L), out_shape=(jax....  125 us
    unnamed x4, local copies, waits for them, and re-layouts  4.01 us
    convert_element_type x1, other arithmetic, per_device(): rot = rotation.astype(BF16)  3.71 us

profile of v2, /device:TPU:29, one launch (start us, length us, event | category | flops | bytes accessed | tf_op | source)
XLA Modules:
  0.0 136.3 jit_solution(7125123149680828267)
XLA Ops:
  0.6 0.7 pad_convert_fusion
  1.3 0.7 convert_bitcast_fusion
  2.0 0.7 broadcast_in_dim.15.matv
  2.6 0.8 broadcast_in_dim.14.mask
  3.5 3.7 %convert_element_type.9.rot = bf16[8192,128]{1,0:T(8,128)(2,1)} convert(f32[8192,128]{1,0:T(8,128)} %param.7) | non-fusion elementwise | flops 1048576 | bytes 6291456 | tf_op jit(solution)/shard_map/convert_element_type | solution.py:333
  7.2 125.1 %shard_map.68 = (bf16[512,2048]{1,0:T(8,128)(2,1)}, f32[1024,128]{1,0:T(8,128)}) custom-call(bf16[512,2048]{1,0:T(8,128)(2,1)} %hid.1, bf16[512,2048]{1,0:T(8,128)(2,1)} %cot.1, bf16[8192,128]{1,0:T(8,128)(2,1)} %convert_element_type.9.rot, f32[512,128]{1,0:T(8,128)} %broadcast_in_dim.14.mask, f32[8,128]{1,0:T(8,128)} %broadcast_in_dim.15.matv, s32[4]{0:T(128)} %match.1), custom_call_target="tpu_custom_call" | custom-call | tf_op jit(solution)/shard_map/pallas_call | solution.py:338
  132.3 0.0 copy-start
  132.3 3.2 %copy.9 = bf16[512,2048]{1,0:T(8,128)(2,1)} copy(bf16[512,2048]{1,0:T(8,128)(2,1)} %get-tuple-element.4) | data formatting | bytes 4194304
  135.5 0.0 copy-done
  135.5 0.8 copy.10
Async XLA Ops:
  132.3 3.2 %copy-start = (f32[1024,128]{1,0:T(8,128)S(1)}, f32[1024,128]{1,0:T(8,128)}, u32[]{:S(2)}) copy-start(f32[1024,128]{1,0:T(8,128)} %get-tuple-element.5) | copy-start | bytes 1572868

commit v3 on v2

--- a/solution.py
+++ b/solution.py
@@ -15,7 +15,7 @@
     R, T, H, lr, L, hid, cot, rot, mask, matv, match, out, grad,
     x, w, part, prec, pfull, pfrec, own, gath, matg, upd, updt, gkeep, gsend, yrec, zsend, zrec, fin, frec,
     lsem, psem, rsend, rrecv, msend, mrecv, psend, precv, qsem, asend, arecv, usend, urecv,
-    ysend, yrecv, zsem, zrsem, fsem,
+    ysend, yrecv, zsem, zrsem, fsem, hold, hsem, gsem,
 ):
     q = R // T
     n, F = hid.shape
@@ -278,7 +278,21 @@
             zsend_of(p, h).start()
 
     def move(h):
-        return remote(fin.at[h], frec.at[h], fsem.at[0, h], fsem.at[1, h], j * q + b, a)
+        if h % 2 == 0:
+            return remote(fin.at[h], hold.at[a, h], fsem.at[0, h], hsem.at[a, h], j * q + b, j)
+        return remote(fin.at[h], hold.at[j, h], fsem.at[0, h], hsem.at[j, h], r, a)
+
+    def hand(p, h):
+        dr, dj = (r, p) if h % 2 == 0 else (p * q + b, j)
+        return remote(hold.at[p, h], frec.at[h], gsem.at[p, h], fsem.at[1, h], dr, dj)
+
+    def relay(h):
+        @pl.when(a == j)
+        def _():
+            for k in range(1, T):
+                p = other(a, k, T)
+                remote(fin.at[h], hold.at[p, h], fsem.at[0, h], hsem.at[p, h], p * q + b, j).wait_recv()
+                hand(p, h).start()
 
     def total(h):
         v = fin[h]
@@ -300,17 +314,24 @@
             ysum(p, h)
         if h:
             total(h - 1)
+        if h > 1:
+            relay(h - 2)
     total(H - 1)
+    for h in range(max(0, H - 2), H):
+        relay(h)
 
     for h in range(H):
         @pl.when(a != j)
         def _(h=h):
-            move(h).wait()
+            move(h).wait_send()
+            remote(fin.at[h], frec.at[h], fsem.at[0, h], fsem.at[1, h], j * q + b, a).wait_recv()
             grad[pl.ds(h * Sh, Sh), :] = frec[h].T
 
         @pl.when(a == j)
         def _(h=h):
             grad[pl.ds(h * Sh, Sh), :] = fin[h].T
+            for k in range(1, T):
+                hand(other(a, k, T), h).wait_send()
 
     for c in rcopies + mcopies + pcopies + sends + ucopies:
         c.wait_send()
@@ -366,6 +387,7 @@
             dma(T, 2), dma(T, 2), dma(2, 2),
             dma(T, q, 2), dma(R, 2), dma(2, T), dma(T),
             dma(T, q, H), dma(q, T, H), dma(T, H), dma(T, H), dma(2, H),
+            pltpu.VMEM((T, H, C, S // H), F32), dma(T, H), dma(T, H),
         ],
         compiler_params=pltpu.CompilerParams(
             collective_id=0, has_side_effects=True, vmem_limit_bytes=60 * 1024 * 1024

time: 137 us -> 137 us (level)
  no operation moved by 1% of the time
where the time goes in v3:
time: 137 us
  Pallas kernels  125 us (91%)
  local copies, waits for them, and re-layouts  5.51 us (4%)
  other arithmetic  5.05 us (4%)
    pallas_call x1, Pallas kernels, per_device(): pl.pallas_call(functools.partial(kernel, R, T, H, lr, L), out_shape=(jax....  125 us
    unnamed x4, local copies, waits for them, and re-layouts  4.01 us
    convert_element_type x1, other arithmetic, per_device(): rot = rotation.astype(BF16)  3.71 us

profile of v3, /device:TPU:29, one launch (start us, length us, event | category | flops | bytes accessed | tf_op | source)
XLA Modules:
  0.0 136.6 jit_solution(14455560911071365736)
XLA Ops:
  0.6 0.7 pad_convert_fusion
  1.3 0.7 convert_bitcast_fusion
  2.0 0.7 broadcast_in_dim.15.matv
  2.6 0.8 broadcast_in_dim.14.mask
  3.5 3.7 %convert_element_type.9.rot = bf16[8192,128]{1,0:T(8,128)(2,1)} convert(f32[8192,128]{1,0:T(8,128)} %param.7) | non-fusion elementwise | flops 1048576 | bytes 6291456 | tf_op jit(solution)/shard_map/convert_element_type | solution.py:354
  7.2 125.4 %shard_map.68 = (bf16[512,2048]{1,0:T(8,128)(2,1)}, f32[1024,128]{1,0:T(8,128)}) custom-call(bf16[512,2048]{1,0:T(8,128)(2,1)} %hid.1, bf16[512,2048]{1,0:T(8,128)(2,1)} %cot.1, bf16[8192,128]{1,0:T(8,128)(2,1)} %convert_element_type.9.rot, f32[512,128]{1,0:T(8,128)} %broadcast_in_dim.14.mask, f32[8,128]{1,0:T(8,128)} %broadcast_in_dim.15.matv, s32[4]{0:T(128)} %match.1), custom_call_target="tpu_custom_call" | custom-call | tf_op jit(solution)/shard_map/pallas_call | solution.py:359
  132.6 0.0 copy-start
  132.6 3.2 %copy.9 = bf16[512,2048]{1,0:T(8,128)(2,1)} copy(bf16[512,2048]{1,0:T(8,128)(2,1)} %get-tuple-element.4) | data formatting | bytes 4194304
  135.8 0.0 copy-done
  135.8 0.8 copy.10
Async XLA Ops:
  132.6 3.2 %copy-start = (f32[1024,128]{1,0:T(8,128)S(1)}, f32[1024,128]{1,0:T(8,128)}, u32[]{:S(2)}) copy-start(f32[1024,128]{1,0:T(8,128)} %get-tuple-element.5) | copy-start | bytes 1572868
